TPU v7x, 128 devices: a whole 4x4x4 slice. The times are simulated.
128 devices in a mesh: batch: 8 (over y_lo, z), tensor: 16 (over y_hi, x, core).
Axes of the slice: x: 4, y: 4 (y_hi: 2, y_lo: 2; y = y_hi * 2 + y_lo), z: 4, core: 2. Of those that a mesh axis runs over, the one named last changes fastest.
Arguments:
- attn_values: bfloat16 [2048, 8192], P('batch', 'tensor'), may hold values from -6 to 6
- out_weight: bfloat16 [8192, 8192], P('tensor'), may hold values from -0.09375 to 0.09375
- residual_t: bfloat16 [8192, 2048], P('tensor', 'batch'), may hold values from -6 to 6
- projector: bfloat16 [8192, 4096], P('tensor'), may hold values from -0.0625 to 0.0625
- student_input: bfloat16 [2048, 4096], P('batch', 'tensor'), may hold values from -6 to 6
- norm_gain: float32 [4096], replicated, may hold values from 0.1 to 1.9
- w_gate: bfloat16 [4096, 8192], P('batch', 'tensor'), may hold values from -0.09375 to 0.09375
- w_up: bfloat16 [4096, 8192], P('batch', 'tensor'), may hold values from -0.09375 to 0.09375
- w_down: bfloat16 [4096, 8192], P('batch', 'tensor'), may hold values from -0.0625 to 0.0625
- route_index: int32 [8, 64], P('batch'), may hold values from -1 to 255, as said below
Outputs:
- teacher_hidden: bfloat16 [8192, 2048], P('tensor', 'batch')
- grad_gate: float32 [4096, 8192], P('batch', 'tensor')
- grad_up: float32 [4096, 8192], P('batch', 'tensor')
- grad_down: float32 [4096, 8192], P('batch', 'tensor')
Inputs may be any that keep to these rules, and one draw needn't show every extreme that they name: `route_index`: in each batch group the live slots come first, hold distinct positions in increasing order, and the empty slots after them hold -1. The batch groups hold 256 live slots together, and some batch group has all 64 slots live.
All inputs are finite; a program needn't handle non-finite values.
Results may differ from a plain program's by a relative error of at most 0.025.
Values may be sent and summed in bfloat16 or wider, within the bound.
No kernel may reach another device: no remote copies, remote signals or barrier semaphores. Data moves between devices by JAX's collectives and lax.ppermute only.
A program may use at most 128 MiB of HBM per device.

v0:
```python
import math
import jax
import jax.numpy as jnp
from jax import lax
from jax.sharding import Mesh
from jax.sharding import PartitionSpec as P

TENSOR = ("tensor_0", "tensor_1", "tensor_2")
epsilon = 1e-05


def from_everyone(value, axis):
    copies = jnp.broadcast_to(value, (lax.axis_size(axis), *value.shape))
    return lax.all_to_all(copies, axis, split_axis=0, concat_axis=0, tiled=True)


def joined_along(blocks, dim):
    lengths = list(blocks.shape[1:])
    lengths[dim] *= blocks.shape[0]
    return jnp.moveaxis(blocks, 0, dim).reshape(lengths)


def collect(value, axis, dim):
    blocks = from_everyone(value, axis)
    return joined_along(blocks, dim)


def side_by_side(arrays, axis, dim, along):
    ends, at = ([], 0)
    for a in arrays[:-1]:
        at += a.shape[along]
        ends.append(at)
    both = jnp.concatenate(arrays, axis=along)
    return tuple(jnp.split(lax.all_gather(both, axis, axis=dim, tiled=True), ends, axis=along))


def cut_along(value, dim, devices):
    lengths = value.shape
    blocks = value.reshape(*lengths[:dim], devices, lengths[dim] // devices, *lengths[dim + 1 :])
    return jnp.moveaxis(blocks, dim, 0)


def sent_and_summed(value, axis, dim):
    devices = lax.axis_size(axis)
    blocks = lax.all_to_all(cut_along(value, dim, devices), axis, 0, 0, tiled=True)
    return jnp.sum(blocks.astype(jnp.float32), axis=0)


def summed_rows(value, axes, dim):
    far, near = axes
    own = sent_and_summed(cut_along(value, dim, lax.axis_size(far)), near, dim + 1)
    return jnp.sum(
        lax.all_to_all(own.astype(jnp.bfloat16), far, 0, 0, tiled=True).astype(jnp.float32), axis=0
    )


def filled_up(lines, devices):
    spare = -len(lines) % devices
    return jnp.pad(lines, [(0, spare)] + [(0, 0)] * (lines.ndim - 1))


def gather_axes(value, axes, dim):
    far, near = axes
    blocks = from_everyone(from_everyone(value, far), near)
    return joined_along(blocks.swapaxes(0, 1).reshape(-1, *value.shape), dim)


def total_of(value, axes):
    lines = value.reshape(-1, value.shape[-1])
    own = summed_rows(filled_up(lines, lax.axis_size(axes[0]) * lax.axis_size(axes[1])), axes, 0)
    whole = gather_axes(own.astype(jnp.bfloat16), axes, 0)
    return whole[: len(lines)].reshape(value.shape).astype(jnp.float32)


def grouped_product(left, right):
    dims = (((1,), (1,)), ((0,), (0,)))
    full = lax.dot_general(left, right, dims, preferred_element_type=jnp.float32)
    rounded = lax.optimization_barrier(full.astype(jnp.bfloat16))
    return jnp.sum(rounded.astype(jnp.float32), axis=0)


def on_device(
    attn_values,
    out_weight,
    residual_t,
    projector,
    student_input,
    norm_gain,
    w_gate,
    w_up,
    w_down,
    route_index,
):
    summed = lax.psum_scatter(
        lax.dot_general(
            out_weight, attn_values, (((0,), (1,)), ((), ())), preferred_element_type=jnp.float32
        ).astype(jnp.bfloat16),
        TENSOR,
        scatter_dimension=0,
        tiled=True,
    ).astype(jnp.float32)
    teacher_hidden = (residual_t.astype(jnp.float32) + summed).astype(jnp.bfloat16)
    slot_pos = route_index[0]
    present = slot_pos >= 0
    safe_slot = jnp.maximum(slot_pos, 0)
    routed_teacher = jnp.where(present[None, :], jnp.take(teacher_hidden, safe_slot, axis=1), 0)
    target_part = lax.dot_general(
        routed_teacher, projector, (((0,), (0,)), ((), ())), preferred_element_type=jnp.float32
    )
    local_rows = jnp.where(present[:, None], jnp.take(student_input, safe_slot, axis=0), 0)
    routed_input = collect(local_rows, TENSOR, 1).astype(jnp.float32)
    mean_square = jnp.mean(routed_input * routed_input, axis=1, keepdims=True)
    normed = (routed_input * lax.rsqrt(mean_square + epsilon) * norm_gain[None, :]).astype(
        jnp.bfloat16
    )
    slot_total = normed.shape[0]
    local_units = w_gate.shape[1]
    gate_full, up_full, down_full = side_by_side((w_gate, w_up, w_down), "batch", 0, 1)
    gate_act = jnp.dot(normed, gate_full, preferred_element_type=jnp.float32)
    up_act = jnp.dot(normed, up_full, preferred_element_type=jnp.float32)
    sigma_gate = jax.nn.sigmoid(gate_act)
    hidden = (gate_act * sigma_gate * up_act).astype(jnp.bfloat16)
    out_part = lax.dot_general(
        hidden, down_full, (((1,), (1,)), ((), ())), preferred_element_type=jnp.float32
    )
    misfit = total_of(
        (out_part - target_part).astype(jnp.bfloat16), (("tensor_0", "tensor_1"), "tensor_2")
    )
    group_count = lax.axis_size("batch")
    mean_routed = student_input.shape[0] // 8
    loss_scale = 1.0 / math.sqrt(mean_routed * group_count)
    grad_out = (jnp.where(present[:, None], misfit, 0.0) * loss_scale).astype(jnp.bfloat16)
    grad_hidden = jnp.dot(grad_out, down_full, preferred_element_type=jnp.float32)
    grad_gate_act = (
        grad_hidden * up_act * sigma_gate * (1.0 + gate_act * (1.0 - sigma_gate))
    ).astype(jnp.bfloat16)
    grad_up_act = (grad_hidden * gate_act * sigma_gate).astype(jnp.bfloat16)
    rows_local = w_gate.shape[0]
    every_normed, every_grad = (
        lax.all_to_all(normed, "batch", split_axis=1, concat_axis=0, tiled=True),
        lax.all_to_all(grad_out, "batch", split_axis=1, concat_axis=0, tiled=True),
    )
    every_gate, every_up, every_hidden = side_by_side(
        (grad_gate_act, grad_up_act, hidden), "batch", 0, 1
    )
    normed_groups = every_normed.reshape(group_count, slot_total, rows_local)
    grad_groups = every_grad.reshape(group_count, slot_total, rows_local)
    gate_groups = every_gate.reshape(group_count, slot_total, local_units)
    up_groups = every_up.reshape(group_count, slot_total, local_units)
    hidden_groups = every_hidden.reshape(group_count, slot_total, local_units)
    grad_gate = grouped_product(normed_groups, gate_groups)
    grad_up = grouped_product(normed_groups, up_groups)
    grad_down = grouped_product(grad_groups, hidden_groups)
    return (teacher_hidden, grad_gate, grad_up, grad_down)


def solution(mesh):
    split = Mesh(
        mesh.devices.reshape(mesh.shape["batch"], 2, 4, 2),
        ("batch", "tensor_0", "tensor_1", "tensor_2"),
    )
    in_specs = (
        P("batch", TENSOR),
        P(TENSOR, None),
        P(TENSOR, "batch"),
        P(TENSOR, None),
        P("batch", TENSOR),
        P(),
        P("batch", TENSOR),
        P("batch", TENSOR),
        P("batch", TENSOR),
        P("batch", None),
    )
    out_specs = (P(TENSOR, "batch"), P("batch", TENSOR), P("batch", TENSOR), P("batch", TENSOR))
    return jax.shard_map(
        on_device, mesh=split, in_specs=in_specs, out_specs=out_specs, check_vma=False
    )
```

profile of v0, /device:TPU:18, one launch (start us, length us, event | category | flops | bytes accessed | tf_op | source)
XLA Modules:
  0.0 288.8 jit_solution(2432564171475395224)
XLA Ops:
  8.1 0.9 copy-done
  9.0 7.7 %convolution_convert_fusion = bf16[8192,256]{1,0:T(8,128)(2,1)} fusion(bf16[512,8192]{1,0:T(8,128)(2,1)} %param.11, bf16[256,512]{1,0:T(8,128)(2,1)S(1)} %copy-done), kind=kOutput, calls=%fused_computation.2 | convolution fusion | flops 2149580800 | bytes 12845056 | tf_op jit(solution)/shard_map/dot_general | solution.py:95
  16.8 0.9 copy-done.7
  18.0 1.3 pad_maximum_fusion
  20.3 14.8 %all_to_all.51 = bf16[16,64,256]{2,1,0:T(8,128)(2,1)S(1)} all-to-all(bf16[16,64,256]{2,1,0:T(8,128)(2,1)S(1)} %broadcast_in_dim.78), channel_id=1, replica_groups=mesh['batch'=8,'tensor_0'=2,'tensor_1'=4,'tensor_2'=2] {'tensor_0','tens..., dimensions={0} | all-to-all | bytes 1048576 | tf_op jit(solution)/shard_map/all_to_all | solution.py:14
  35.6 88.8 %reduce-scatter.2.cloned.1.call-done = bf16[512,256]{1,0:T(8,128)(2,1)} async-done(((bf16[8192,256]{1,0:T(8,128)(2,1)}), bf16[512,256]{1,0:T(8,128)(2,1)}) %reduce-scatter.2.cloned.1.call-update) | async-done | bytes 262160 | tf_op jit(solution)/shard_map/reduce_scatter | solution.py:94
  124.4 1.0 add_convert_fusion
  125.6 0.7 gather_fusion.1
  126.3 45.2 %all-gather.3.cloned.1.call-done = bf16[4096,1536]{1,0:T(8,128)(2,1)} async-done(((bf16[512,1536]{1,0:T(8,128)(2,1)}), bf16[4096,1536]{1,0:T(8,128)(2,1)}) %all-gather.3.cloned.1.call-update) | async-done | bytes 12582928 | tf_op jit(solution)/shard_map/all_gather | solution.py:34
  171.5 3.1 %fusion.3 = f32[64,512]{1,0:T(8,128)S(1)} fusion(bf16[4096,1536]{1,0:T(8,128)(2,1)} %all-gather.3.cloned.1.call-done, f32[64,4096]{1,0:T(8,128)S(1)} %bitcast.38, f32[4096]{0:T(1024)S(1)} %copy-done.11, f32[64]{0:T(128)S(1)} %add_rsqrt_fusion), kind=kOutput, calls=%fused_computation.10 | convolution fusion | flops 269221888 | bytes 5390592 | tf_op jit(solution)/shard_map/dot_general | solution.py:119
  174.6 3.7 %multiply_convert_fusion.5 = (bf16[64,512]{1,0:T(8,128)(2,1)S(1)}, f32[64,512]{1,0:T(8,128)}) fusion(f32[64,512]{1,0:T(8,128)S(1)} %fusion.3, bf16[4096,1536]{1,0:T(8,128)(2,1)} %all-gather.3.cloned.1.call-done, f32[64,4096]{1,0:T(8,128)S(1)} %bitcast.39, f32[4096]{0:T(1024)S(1)} %copy-done.11, f32[64]{0:T(128)S(1)} %add_rsqrt_fusion), kind=kOutput, calls=%fused_computation.44 | convolution fusion | flops 269418496 | bytes 5587200 | tf_op jit(solution)/shard_map/dot_general | solution.py:120
  178.3 3.7 %fusion.7 = f32[64,4096]{1,0:T(8,128)S(1)} fusion(bf16[64,512]{1,0:T(8,128)(2,1)S(1)} %get-tuple-element.13, bf16[4096,1536]{1,0:T(8,128)(2,1)} %all-gather.3.cloned.1.call-done), kind=kOutput, calls=%fused_computation.14 | convolution fusion | flops 268435456 | bytes 5308416 | tf_op jit(solution)/shard_map/dot_general | solution.py:123
  182.1 0.9 fusion
  183.4 4.2 %all_to_all.52 = bf16[2,8,4,4096]{3,2,1,0:T(4,128)(2,1)S(1)} all-to-all(bf16[2,8,4,4096]{3,2,1,0:T(4,128)(2,1)S(1)} %bitcast.37), channel_id=1, replica_groups=mesh['batch'=8,'tensor_0'=2,'tensor_1'=4,'tensor_2'=2] {'tensor_2'}, dimensions={0} | all-to-all | bytes 1048576 | tf_op jit(solution)/shard_map/all_to_all | solution.py:45
  188.0 12.5 %all_to_all.53 = bf16[8,4,4096]{2,1,0:T(4,128)(2,1)S(1)} all-to-all(bf16[8,4,4096]{2,1,0:T(4,128)(2,1)S(1)} %reduce_sum.61), channel_id=1, replica_groups=mesh['batch'=8,'tensor_0'=2,'tensor_1'=4,'tensor_2'=2] {'tensor_0','tens..., dimensions={0} | all-to-all | bytes 524288 | tf_op jit(solution)/shard_map/all_to_all | solution.py:53
  200.8 11.3 %all_to_all.54 = bf16[8,4,4096]{2,1,0:T(4,128)(2,1)S(1)} all-to-all(bf16[8,4,4096]{2,1,0:T(4,128)(2,1)S(1)} %broadcast_in_dim.84), channel_id=1, replica_groups=mesh['batch'=8,'tensor_0'=2,'tensor_1'=4,'tensor_2'=2] {'tensor_0','tens..., dimensions={0} | all-to-all | bytes 524288 | tf_op jit(solution)/shard_map/all_to_all | solution.py:14
  212.3 4.2 %all_to_all.55 = bf16[2,8,4,4096]{3,2,1,0:T(4,128)(2,1)S(1)} all-to-all(bf16[2,8,4,4096]{3,2,1,0:T(4,128)(2,1)S(1)} %broadcast_in_dim.85), channel_id=1, replica_groups=mesh['batch'=8,'tensor_0'=2,'tensor_1'=4,'tensor_2'=2] {'tensor_2'}, dimensions={0} | all-to-all | bytes 1048576 | tf_op jit(solution)/shard_map/all_to_all | solution.py:14
  217.0 3.1 %multiply_convert_fusion.4 = (bf16[64,512]{1,0:T(8,128)(2,1)S(1)}, bf16[64,512]{1,0:T(8,128)(2,1)S(1)}) fusion(f32[64,512]{1,0:T(8,128)S(1)} %fusion.3, f32[64,512]{1,0:T(8,128)} %get-tuple-element.14, bf16[4096,1536]{1,0:T(8,128)(2,1)} %all-gather.3.cloned.1.call-done, f32[64,4096]{1,0:T(8,128)S(1)} %reshape.96, pred[64]{0:T(512)(128)(4,1)S(1)} %get-tuple-element.11), kind=kOutput, calls=%fused_computation.43 | convolution fusion | flops 269647872 | bytes 5636160 | tf_op jit(solution)/shard_map/dot_general | solution.py:133
  221.8 1.4 fusion.13
  223.2 3.7 %all-to-all-start.1 = ((bf16[64,8,512]{2,0,1:T(8,128)(2,1)}), bf16[64,8,512]{2,0,1:T(8,128)(2,1)S(1)}, u32[]{:S(2)}, u32[]{:S(2)}) async-start(bf16[64,8,512]{2,0,1:T(8,128)(2,1)} %fusion.13), calls=%async_computation.2 | async-start | bytes 1048576 | tf_op jit(solution)/shard_map/all_to_all | solution.py:140
  226.8 0.7 reshape.97
  227.6 1.4 fusion.11
  229.0 32.2 %all-gather.5.cloned.1.call-done = bf16[512,1536]{1,0:T(8,128)(2,1)} async-done(((bf16[64,1536]{1,0:T(8,128)(2,1)}), bf16[512,1536]{1,0:T(8,128)(2,1)}) %all-gather.5.cloned.1.call-update) | async-done | bytes 1572880 | tf_op jit(solution)/shard_map/all_gather | solution.py:34
  261.2 1.5 fusion.30
  262.7 4.0 %all-to-all-start.6 = ((bf16[64,8,512]{2,0,1:T(8,128)(2,1)}), bf16[64,8,512]{2,0,1:T(8,128)(2,1)S(1)}, u32[]{:S(2)}, u32[]{:S(2)}) async-start(bf16[64,8,512]{2,0,1:T(8,128)(2,1)} %fusion.11), calls=%async_computation.7 | async-start | bytes 1048576 | tf_op jit(solution)/shard_map/all_to_all | solution.py:141
  266.7 3.2 %convolution_convert_fusion.2 = bf16[8,512,512]{2,1,0:T(8,128)(2,1)} fusion(bf16[8,64,512]{2,1,0:T(8,128)(2,1)S(1)} %bitcast.36, bf16[64,8,512]{2,0,1:T(8,128)(2,1)S(1)} %all-to-all-done.1), kind=kOutput, calls=%fused_computation.17 | convolution fusion | flops 270532608 | bytes 5242880 | tf_op jit(solution)/shard_map/dot_general | solution.py:77
  270.0 3.3 %convolution_convert_fusion.3 = bf16[8,512,512]{2,1,0:T(8,128)(2,1)} fusion(bf16[8,64,512]{2,1,0:T(8,128)(2,1)S(1)} %bitcast.35, bf16[64,8,512]{2,0,1:T(8,128)(2,1)S(1)} %all-to-all-done.1), kind=kOutput, calls=%fused_computation.18 | convolution fusion | flops 270532608 | bytes 5242880 | tf_op jit(solution)/shard_map/dot_general | solution.py:77
  273.2 1.8 all-to-all-done.6
  275.0 1.3 convolution_convert_fusion.1
  276.3 1.6 convert_reduce_fusion
  277.9 0.9 copy-done.3
  278.9 2.5 convert_reduce_fusion.1
  (54 shorter events, 5.5 us)
Async XLA Ops:
  8.0 1.0 copy-start
  8.0 116.4 %reduce-scatter.2.cloned.1.call-start = ((), (), s32[]{:S(2)}) async-start(), calls=%async_computation.8 | async-start | bytes 4456448 | tf_op jit(solution)/shard_map/reduce_scatter | solution.py:94
  16.7 1.0 copy-start.7
  16.7 1.2 copy-start.8
  16.7 1.4 copy-start.9
  16.7 2.7 copy-start.12
  16.7 2.7 copy-start.6
  16.7 154.8 %all-gather.3.cloned.1.call-start = ((), (), s32[]{:S(2)}) async-start(), calls=%async_computation.9 | async-start | bytes 14155776 | tf_op jit(solution)/shard_map/all_gather | solution.py:34
  19.3 105.1 %copy-start.10 = (bf16[512,256]{1,0:T(8,128)(2,1)S(1)}, bf16[512,256]{1,0:T(8,128)(2,1)}, u32[]{:S(2)}) copy-start(bf16[512,256]{1,0:T(8,128)(2,1)} %param.12) | copy-start | bytes 786436
  19.3 241.9 %all-gather.5.cloned.1.call-start = ((), (), s32[]{:S(2)}) async-start(), calls=%async_computation.10 | async-start | bytes 1769472 | tf_op jit(solution)/shard_map/all_gather | solution.py:34
  20.3 151.2 %copy-start.11 = (f32[4096]{0:T(1024)S(1)}, f32[4096]{0:T(1024)}, u32[]{:S(2)}) copy-start(f32[4096]{0:T(1024)} %param.15) | copy-start | bytes 49156
  125.4 52.9 %copy-start.5 = (bf16[512,256]{1,0:T(8,128)(2,1)}, bf16[512,256]{1,0:T(8,128)(2,1)S(1)}, u32[]{:S(2)}) copy-start(bf16[512,256]{1,0:T(8,128)(2,1)S(1)} %add_convert_fusion) | copy-start | bytes 786436
  178.3 3.7 %copy-start.4 = (bf16[512,4096]{1,0:T(8,128)(2,1)S(1)}, bf16[512,4096]{1,0:T(8,128)(2,1)}, u32[]{:S(2)}) copy-start(bf16[512,4096]{1,0:T(8,128)(2,1)} %param.13) | copy-start | bytes 12582916
  223.2 39.5 %all-to-all-start.1 = ((bf16[64,8,512]{2,0,1:T(8,128)(2,1)}), bf16[64,8,512]{2,0,1:T(8,128)(2,1)S(1)}, u32[]{:S(2)}, u32[]{:S(2)}) async-start(bf16[64,8,512]{2,0,1:T(8,128)(2,1)} %fusion.13), calls=%async_computation.2 | async-start | bytes 1048576 | tf_op jit(solution)/shard_map/all_to_all | solution.py:140
  262.7 12.3 %all-to-all-start.6 = ((bf16[64,8,512]{2,0,1:T(8,128)(2,1)}), bf16[64,8,512]{2,0,1:T(8,128)(2,1)S(1)}, u32[]{:S(2)}, u32[]{:S(2)}) async-start(bf16[64,8,512]{2,0,1:T(8,128)(2,1)} %fusion.11), calls=%async_computation.7 | async-start | bytes 1048576 | tf_op jit(solution)/shard_map/all_to_all | solution.py:141
  275.0 2.9 %copy-start.2 = (bf16[8,512,512]{2,1,0:T(8,128)(2,1)S(1)}, bf16[8,512,512]{2,1,0:T(8,128)(2,1)}, u32[]{:S(2)}) copy-start(bf16[8,512,512]{2,1,0:T(8,128)(2,1)} %convolution_convert_fusion.2) | copy-start | bytes 12582916
  275.0 3.8 %copy-start.3 = (bf16[8,512,512]{2,1,0:T(8,128)(2,1)S(1)}, bf16[8,512,512]{2,1,0:T(8,128)(2,1)}, u32[]{:S(2)}) copy-start(bf16[8,512,512]{2,1,0:T(8,128)(2,1)} %convolution_convert_fusion.3) | copy-start | bytes 12582916
  276.3 5.0 %copy-start.1 = (bf16[256,512]{1,0:T(8,128)(2,1)S(1)}, bf16[256,512]{1,0:T(8,128)(2,1)}, u32[]{:S(2)}) copy-start(bf16[256,512]{1,0:T(8,128)(2,1)} %param.10) | copy-start | bytes 786436
Sparse Core Ops, SparseCore 0:
  16.8 107.5 reduce-scatter.1
Sparse Core Ops, SparseCore 1:
  19.4 152.1 all-gather.2
  220.9 40.3 all-gather.4
where the time goes:
time: 289 us
  waiting for transfers between devices  168 us (58%)
  blocking collectives  46.9 us (16%)
  matrix products  30 us (10%)
  between operations  15.8 us (5%)
  other arithmetic  11.1 us (4%)
  local copies, waits for them, and re-layouts  9.04 us (3%)
  starting transfers between devices  7.83 us (3%)
    reduce_scatter x1, waiting for transfers between devices, on_device(): lax.psum_scatter(lax.dot_general(out_weight, attn_values, (((0,), (1,)),...  88.8 us
    all_gather x2, waiting for transfers between devices, side_by_side(): lax.all_gather(both, axis, axis=dim, tiled=True)  77.5 us
    all_to_all x3, blocking collectives, from_everyone(): return lax.all_to_all(copies, axis, split_axis=0, concat_axis=0, tiled=True)  30.2 us
    all_to_all x1, blocking collectives, summed_rows(): lax.all_to_all(own.astype(jnp.bfloat16), far, 0, 0, tiled=True)  12.5 us
    dot_general x3, matrix products, grouped_product(): lax.dot_general(left, right, dims, preferred_element_type=jnp.float32)  7.81 us
    dot_general x1, matrix products, on_device(): lax.dot_general(out_weight, attn_values, (((0,), (1,)), ((), ())), prefer...  7.72 us
  transfers between devices with their start and end apart: 5, of which 4 were waited for; matrix products, arithmetic and copies ran while one was open for 6% of the time, Pallas kernels for 0%

commit v1 on v0

--- a/solution.py
+++ b/solution.py
@@ -138,7 +138,12 @@
     rows_local = w_gate.shape[0]
     every_normed, every_grad = (
         lax.all_to_all(normed, "batch", split_axis=1, concat_axis=0, tiled=True),
-        lax.all_to_all(grad_out, "batch", split_axis=1, concat_axis=0, tiled=True),
+        jnp.concatenate(
+            lax.all_to_all(
+                jnp.stack(jnp.split(grad_out, lax.axis_size("batch"), axis=1)), "batch", 0, 0
+            ),
+            axis=0,
+        ),
     )
     every_gate, every_up, every_hidden = side_by_side(
         (grad_gate_act, grad_up_act, hidden), "batch", 0, 1

time: 289 us -> 290 us (level)
  local copies, waits for them, and re-layouts: 9.04 us -> 13.4 us
  waiting for transfers between devices: 168 us -> 165 us
    unnamed x26 -> x39, local copies, waits for them, and re-layouts: 3.15 us -> 7.6 us
  transfers between devices with their start and end apart: 5 -> 5, of which waited for: 4 -> 4; matrix products, arithmetic and copies ran while one was open for 6% -> 7% of each run, Pallas kernels for 0% -> 0%
where the time goes in v1:
time: 290 us; the launch traced here: 289 us
  waiting for transfers between devices  165 us (57%)
  blocking collectives  47 us (16%)
  matrix products  30 us (10%)
  between operations  15.8 us (5%)
  local copies, waits for them, and re-layouts  13.4 us (5%)
  other arithmetic  9.85 us (3%)
  starting transfers between devices  7.65 us (3%)
    reduce_scatter x1, waiting for transfers between devices, on_device(): lax.psum_scatter(lax.dot_general(out_weight, attn_values, (((0,), (1,)),...  88.8 us
    all_gather x2, waiting for transfers between devices, side_by_side(): lax.all_gather(both, axis, axis=dim, tiled=True)  74.7 us
    all_to_all x3, blocking collectives, from_everyone(): return lax.all_to_all(copies, axis, split_axis=0, concat_axis=0, tiled=True)  30.4 us
    all_to_all x1, blocking collectives, summed_rows(): lax.all_to_all(own.astype(jnp.bfloat16), far, 0, 0, tiled=True)  12.5 us
    dot_general x3, matrix products, grouped_product(): lax.dot_general(left, right, dims, preferred_element_type=jnp.float32)  7.8 us
    dot_general x1, matrix products, on_device(): lax.dot_general(out_weight, attn_values, (((0,), (1,)), ((), ())), prefer...  7.72 us
    unnamed x39, local copies, waits for them, and re-layouts  7.6 us
  transfers between devices with their start and end apart: 5, of which 4 were waited for; matrix products, arithmetic and copies ran while one was open for 7% of the time, Pallas kernels for 0%

profile of v1, /device:TPU:18, one launch (start us, length us, event | category | flops | bytes accessed | tf_op | source)
XLA Modules:
  0.0 289.1 jit_solution(9378865586707072909)
XLA Ops:
  8.1 0.9 copy-done
  9.0 7.7 %convolution_convert_fusion = bf16[8192,256]{1,0:T(8,128)(2,1)} fusion(bf16[512,8192]{1,0:T(8,128)(2,1)} %param.11, bf16[256,512]{1,0:T(8,128)(2,1)S(1)} %copy-done), kind=kOutput, calls=%fused_computation.2 | convolution fusion | flops 2149580800 | bytes 12845056 | tf_op jit(solution)/shard_map/dot_general | solution.py:95
  16.8 0.9 copy-done.7
  18.0 1.3 pad_maximum_fusion
  19.4 0.7 gather_fusion
  20.3 14.8 %all_to_all.43 = bf16[16,64,256]{2,1,0:T(8,128)(2,1)S(1)} all-to-all(bf16[16,64,256]{2,1,0:T(8,128)(2,1)S(1)} %broadcast_in_dim.74), channel_id=1, replica_groups=mesh['batch'=8,'tensor_0'=2,'tensor_1'=4,'tensor_2'=2] {'tensor_0','tens..., dimensions={0} | all-to-all | bytes 1048576 | tf_op jit(solution)/shard_map/all_to_all | solution.py:14
  35.6 88.8 %reduce-scatter.2.cloned.1.call-done = bf16[512,256]{1,0:T(8,128)(2,1)} async-done(((bf16[8192,256]{1,0:T(8,128)(2,1)}), bf16[512,256]{1,0:T(8,128)(2,1)}) %reduce-scatter.2.cloned.1.call-update) | async-done | bytes 262160 | tf_op jit(solution)/shard_map/reduce_scatter | solution.py:94
  124.4 1.0 add_convert_fusion
  125.6 0.7 gather_fusion.1
  126.3 45.2 %all-gather.3.cloned.1.call-done = bf16[4096,1536]{1,0:T(8,128)(2,1)} async-done(((bf16[512,1536]{1,0:T(8,128)(2,1)}), bf16[4096,1536]{1,0:T(8,128)(2,1)}) %all-gather.3.cloned.1.call-update) | async-done | bytes 12582928 | tf_op jit(solution)/shard_map/all_gather | solution.py:34
  171.5 3.1 %fusion.3 = f32[64,512]{1,0:T(8,128)S(1)} fusion(bf16[4096,1536]{1,0:T(8,128)(2,1)} %all-gather.3.cloned.1.call-done, f32[64,4096]{1,0:T(8,128)S(1)} %bitcast.69, f32[4096]{0:T(1024)S(1)} %copy-done.11, f32[64]{0:T(128)S(1)} %add_rsqrt_fusion), kind=kOutput, calls=%fused_computation.10 | convolution fusion | flops 269221888 | bytes 5390592 | tf_op jit(solution)/shard_map/dot_general | solution.py:119
  174.6 3.8 %multiply_convert_fusion.4 = (bf16[64,512]{1,0:T(8,128)(2,1)S(1)}, f32[64,512]{1,0:T(8,128)}) fusion(f32[64,512]{1,0:T(8,128)S(1)} %fusion.3, bf16[4096,1536]{1,0:T(8,128)(2,1)} %all-gather.3.cloned.1.call-done, f32[64,4096]{1,0:T(8,128)S(1)} %bitcast.70, f32[4096]{0:T(1024)S(1)} %copy-done.11, f32[64]{0:T(128)S(1)} %add_rsqrt_fusion), kind=kOutput, calls=%fused_computation.37 | convolution fusion | flops 269418496 | bytes 5587200 | tf_op jit(solution)/shard_map/dot_general | solution.py:120
  178.4 3.7 %fusion.7 = f32[64,4096]{1,0:T(8,128)S(1)} fusion(bf16[64,512]{1,0:T(8,128)(2,1)S(1)} %get-tuple-element.13, bf16[4096,1536]{1,0:T(8,128)(2,1)} %all-gather.3.cloned.1.call-done), kind=kOutput, calls=%fused_computation.14 | convolution fusion | flops 268435456 | bytes 5308416 | tf_op jit(solution)/shard_map/dot_general | solution.py:123
  182.1 0.9 fusion
  183.4 4.2 %all_to_all.44 = bf16[2,8,4,4096]{3,2,1,0:T(4,128)(2,1)S(1)} all-to-all(bf16[2,8,4,4096]{3,2,1,0:T(4,128)(2,1)S(1)} %bitcast.68), channel_id=1, replica_groups=mesh['batch'=8,'tensor_0'=2,'tensor_1'=4,'tensor_2'=2] {'tensor_2'}, dimensions={0} | all-to-all | bytes 1048576 | tf_op jit(solution)/shard_map/all_to_all | solution.py:45
  188.1 12.5 %all_to_all.45 = bf16[8,4,4096]{2,1,0:T(4,128)(2,1)S(1)} all-to-all(bf16[8,4,4096]{2,1,0:T(4,128)(2,1)S(1)} %reduce_sum.61), channel_id=1, replica_groups=mesh['batch'=8,'tensor_0'=2,'tensor_1'=4,'tensor_2'=2] {'tensor_0','tens..., dimensions={0} | all-to-all | bytes 524288 | tf_op jit(solution)/shard_map/all_to_all | solution.py:53
  200.8 11.3 %all_to_all.46 = bf16[8,4,4096]{2,1,0:T(4,128)(2,1)S(1)} all-to-all(bf16[8,4,4096]{2,1,0:T(4,128)(2,1)S(1)} %broadcast_in_dim.80), channel_id=1, replica_groups=mesh['batch'=8,'tensor_0'=2,'tensor_1'=4,'tensor_2'=2] {'tensor_0','tens..., dimensions={0} | all-to-all | bytes 524288 | tf_op jit(solution)/shard_map/all_to_all | solution.py:14
  212.4 4.3 %all_to_all.47 = bf16[2,8,4,4096]{3,2,1,0:T(4,128)(2,1)S(1)} all-to-all(bf16[2,8,4,4096]{3,2,1,0:T(4,128)(2,1)S(1)} %broadcast_in_dim.81), channel_id=1, replica_groups=mesh['batch'=8,'tensor_0'=2,'tensor_1'=4,'tensor_2'=2] {'tensor_2'}, dimensions={0} | all-to-all | bytes 1048576 | tf_op jit(solution)/shard_map/all_to_all | solution.py:14
  217.4 3.0 %multiply_convert_fusion.3 = (bf16[64,512]{1,0:T(8,128)(2,1)S(1)}, bf16[64,512]{1,0:T(8,128)(2,1)S(1)}) fusion(f32[64,512]{1,0:T(8,128)S(1)} %copy-done.14, f32[64,512]{1,0:T(8,128)S(1)} %copy-done.15, bf16[64,4096]{1,0:T(8,128)(2,1)S(1)} %multiply_convert_fusion, bf16[4096,1536]{1,0:T(8,128)(2,1)} %all-gather.3.cloned.1.call-done), kind=kOutput, calls=%fused_computation.36 | convolution fusion | flops 268861440 | bytes 5111808 | tf_op jit(solution)/shard_map/dot_general | solution.py:133
  220.5 0.7 pad_maximum_fusion.1
  222.1 1.4 fusion.11
  223.5 3.5 %all-to-all-start.1 = ((bf16[64,8,512]{2,0,1:T(8,128)(2,1)}), bf16[64,8,512]{2,0,1:T(8,128)(2,1)S(1)}, u32[]{:S(2)}, u32[]{:S(2)}) async-start(bf16[64,8,512]{2,0,1:T(8,128)(2,1)} %fusion.11), calls=%async_computation.2 | async-start | bytes 1048576 | tf_op jit(solution)/shard_map/all_to_all | solution.py:140
  232.1 29.5 %all-gather.5.cloned.1.call-done = bf16[512,1536]{1,0:T(8,128)(2,1)} async-done(((bf16[64,1536]{1,0:T(8,128)(2,1)}), bf16[512,1536]{1,0:T(8,128)(2,1)}) %all-gather.5.cloned.1.call-update) | async-done | bytes 1572880 | tf_op jit(solution)/shard_map/all_gather | solution.py:34
  261.6 1.5 fusion.30
  263.1 4.0 %all-to-all-start.6 = ((bf16[8,64,512]{2,1,0:T(8,128)(2,1)}), bf16[8,64,512]{2,1,0:T(8,128)(2,1)S(1)}, u32[]{:S(2)}, u32[]{:S(2)}) async-start(bf16[8,64,512]{2,1,0:T(8,128)(2,1)} %fusion.14), calls=%async_computation.7 | async-start | bytes 1048576 | tf_op jit(solution)/shard_map/all_to_all | solution.py:142
  267.1 3.2 %convolution_convert_fusion.2 = bf16[8,512,512]{2,1,0:T(8,128)(2,1)} fusion(bf16[8,64,512]{2,1,0:T(8,128)(2,1)S(1)} %bitcast.67, bf16[64,8,512]{2,0,1:T(8,128)(2,1)S(1)} %all-to-all-done.1), kind=kOutput, calls=%fused_computation.17 | convolution fusion | flops 270532608 | bytes 5242880 | tf_op jit(solution)/shard_map/dot_general | solution.py:77
  270.3 3.3 %convolution_convert_fusion.3 = bf16[8,512,512]{2,1,0:T(8,128)(2,1)} fusion(bf16[8,64,512]{2,1,0:T(8,128)(2,1)S(1)} %bitcast.66, bf16[64,8,512]{2,0,1:T(8,128)(2,1)S(1)} %all-to-all-done.1), kind=kOutput, calls=%fused_computation.18 | convolution fusion | flops 270532608 | bytes 5242880 | tf_op jit(solution)/shard_map/dot_general | solution.py:77
  273.6 1.8 all-to-all-done.6
  275.4 1.3 convolution_convert_fusion.1
  276.7 1.6 convert_reduce_fusion
  278.3 0.9 copy-done.3
  279.2 2.5 convert_reduce_fusion.1
  (67 shorter events, 9.4 us)
Async XLA Ops:
  8.0 1.0 copy-start
  8.0 116.4 %reduce-scatter.2.cloned.1.call-start = ((), (), s32[]{:S(2)}) async-start(), calls=%async_computation.8 | async-start | bytes 4456448 | tf_op jit(solution)/shard_map/reduce_scatter | solution.py:94
  16.7 1.0 copy-start.7
  16.7 1.2 copy-start.8
  16.7 1.4 copy-start.9
  16.7 2.7 copy-start.12
  16.7 2.7 copy-start.6
  16.7 154.8 %all-gather.3.cloned.1.call-start = ((), (), s32[]{:S(2)}) async-start(), calls=%async_computation.9 | async-start | bytes 14155776 | tf_op jit(solution)/shard_map/all_gather | solution.py:34
  19.3 105.1 %copy-start.10 = (bf16[512,256]{1,0:T(8,128)(2,1)S(1)}, bf16[512,256]{1,0:T(8,128)(2,1)}, u32[]{:S(2)}) copy-start(bf16[512,256]{1,0:T(8,128)(2,1)} %param.12) | copy-start | bytes 786436
  19.3 242.3 %all-gather.5.cloned.1.call-start = ((), (), s32[]{:S(2)}) async-start(), calls=%async_computation.10 | async-start | bytes 1769472 | tf_op jit(solution)/shard_map/all_gather | solution.py:34
  20.3 151.2 %copy-start.11 = (f32[4096]{0:T(1024)S(1)}, f32[4096]{0:T(1024)}, u32[]{:S(2)}) copy-start(f32[4096]{0:T(1024)} %param.15) | copy-start | bytes 49156
  125.4 53.0 %copy-start.5 = (bf16[512,256]{1,0:T(8,128)(2,1)}, bf16[512,256]{1,0:T(8,128)(2,1)S(1)}, u32[]{:S(2)}) copy-start(bf16[512,256]{1,0:T(8,128)(2,1)S(1)} %add_convert_fusion) | copy-start | bytes 786436
  174.6 7.5 %copy-start.13 = (f32[64,512]{1,0:T(8,128)}, f32[64,512]{1,0:T(8,128)S(1)}, u32[]{:S(2)}) copy-start(f32[64,512]{1,0:T(8,128)S(1)} %fusion.3) | copy-start | bytes 393220
  178.4 3.7 %copy-start.4 = (bf16[512,4096]{1,0:T(8,128)(2,1)S(1)}, bf16[512,4096]{1,0:T(8,128)(2,1)}, u32[]{:S(2)}) copy-start(bf16[512,4096]{1,0:T(8,128)(2,1)} %param.13) | copy-start | bytes 12582916
  212.4 5.1 %copy-start.14 = (f32[64,512]{1,0:T(8,128)S(1)}, f32[64,512]{1,0:T(8,128)}, u32[]{:S(2)}) copy-start(f32[64,512]{1,0:T(8,128)} %copy-done.13) | copy-start | bytes 393220
  212.4 5.0 %copy-start.15 = (f32[64,512]{1,0:T(8,128)S(1)}, f32[64,512]{1,0:T(8,128)}, u32[]{:S(2)}) copy-start(f32[64,512]{1,0:T(8,128)} %get-tuple-element.14) | copy-start | bytes 393220
  223.5 39.5 %all-to-all-start.1 = ((bf16[64,8,512]{2,0,1:T(8,128)(2,1)}), bf16[64,8,512]{2,0,1:T(8,128)(2,1)S(1)}, u32[]{:S(2)}, u32[]{:S(2)}) async-start(bf16[64,8,512]{2,0,1:T(8,128)(2,1)} %fusion.11), calls=%async_computation.2 | async-start | bytes 1048576 | tf_op jit(solution)/shard_map/all_to_all | solution.py:140
  263.1 12.3 %all-to-all-start.6 = ((bf16[8,64,512]{2,1,0:T(8,128)(2,1)}), bf16[8,64,512]{2,1,0:T(8,128)(2,1)S(1)}, u32[]{:S(2)}, u32[]{:S(2)}) async-start(bf16[8,64,512]{2,1,0:T(8,128)(2,1)} %fusion.14), calls=%async_computation.7 | async-start | bytes 1048576 | tf_op jit(solution)/shard_map/all_to_all | solution.py:142
  275.4 2.9 %copy-start.2 = (bf16[8,512,512]{2,1,0:T(8,128)(2,1)S(1)}, bf16[8,512,512]{2,1,0:T(8,128)(2,1)}, u32[]{:S(2)}) copy-start(bf16[8,512,512]{2,1,0:T(8,128)(2,1)} %convolution_convert_fusion.2) | copy-start | bytes 12582916
  275.4 3.8 %copy-start.3 = (bf16[8,512,512]{2,1,0:T(8,128)(2,1)S(1)}, bf16[8,512,512]{2,1,0:T(8,128)(2,1)}, u32[]{:S(2)}) copy-start(bf16[8,512,512]{2,1,0:T(8,128)(2,1)} %convolution_convert_fusion.3) | copy-start | bytes 12582916
  276.7 5.0 %copy-start.1 = (bf16[256,512]{1,0:T(8,128)(2,1)S(1)}, bf16[256,512]{1,0:T(8,128)(2,1)}, u32[]{:S(2)}) copy-start(bf16[256,512]{1,0:T(8,128)(2,1)} %param.10) | copy-start | bytes 786436
Sparse Core Ops, SparseCore 0:
  16.8 107.5 reduce-scatter.1
Sparse Core Ops, SparseCore 1:
  19.4 152.1 all-gather.2
  221.3 40.3 all-gather.4
